TPU v7x, 32 devices: a whole 2x2x4 slice. The times are simulated.
32 devices in a mesh: rows: 8 (over z, x), cols: 4 (over y, core).
Axes of the slice: x: 2, y: 2, z: 4, core: 2. Of those that a mesh axis runs over, the one named last changes fastest.
Arguments:
- query: bfloat16 [24, 256, 2048], P('rows', 'cols'), may hold values from -6 to 6
- key: bfloat16 [24, 256, 2048], P('rows', 'cols'), may hold values from -6 to 6
- value: bfloat16 [24, 256, 2048], P('rows', 'cols'), may hold values from -6 to 6
- cotangent: bfloat16 [24, 256, 2048], P('rows', 'cols'), may hold values from -6 to 6
- conv_weight: bfloat16 [9, 2048], replicated, may hold values from -1.1953125 to 1.1953125
- row_mask: int32 [24, 2, 2], P('rows'), may hold values from 0 to 1, as said below
- col_mask: int32 [256, 3, 3], P('cols'), may hold values from 0 to 1, as said below
Outputs:
- out: bfloat16 [24, 256, 2048], P('rows', 'cols')
- dquery: bfloat16 [24, 256, 2048], P('rows', 'cols')
- dkey: bfloat16 [24, 256, 2048], P('rows', 'cols')
- dvalue: bfloat16 [24, 256, 2048], P('rows', 'cols')
Inputs may be any that keep to these rules, and one draw needn't show every extreme that they name: `row_mask`: every diagonal block is 1: a query block always sees its own block. `col_mask`: every diagonal block is 1: a query block always sees its own block.
All inputs are finite; a program needn't handle non-finite values.
Results may differ from a plain program's by a relative error of at most 0.011.
Values may be sent and summed in bfloat16 or wider, within the bound.
A program may use at most 128 MiB of HBM per device.

v0:
```python
import math

import jax
import jax.numpy as jnp
from jax import lax
from jax.sharding import PartitionSpec as P

HEAD_DIM = 128
SHEET_ROW_BLOCKS = 2
COL_BLOCKS = 3


def padded(array, sides, width):
    for axis, dim in sides:
        devices, length = (lax.axis_size(axis), array.shape[dim])
        up = [(i, (i + 1) % devices) for i in range(devices - 1)]
        down = [(j, i) for i, j in up]
        last = lax.slice_in_dim(array, length - width, length, axis=dim)
        leading = lax.slice_in_dim(array, 0, width, axis=dim)
        before = lax.ppermute(last, axis, up)
        after = lax.ppermute(leading, axis, down)
        array = jnp.concatenate([before, array, after], axis=dim)
    return array


def block_allow(block_mask_table, query_pos, key_pos, block_len, block_count):
    labels = jnp.arange(block_count)
    query_onehot_rows = (query_pos[:, None] // block_len == labels[None, :]).astype(jnp.float32)
    key_onehot_rows = (key_pos[:, None] // block_len == labels[None, :]).astype(jnp.float32)
    merged_links = jnp.einsum(
        "xv,zvs,hs->zxh", query_onehot_rows, block_mask_table.astype(jnp.float32), key_onehot_rows
    )
    return merged_links > 0.5


def line_attention(query_part, key_part, value_part, grad_part, allowed, layout):
    if layout == "bq":
        query_form = "bqhd"
        key_layout_shape = "bkhd"
    else:
        query_form = "qbhd"
        key_layout_shape = "kbhd"
    score_scale = 1.0 / math.sqrt(query_part.shape[-1])
    pair_form = query_form + "," + key_layout_shape + "->bhqk"
    scores = (
        jnp.einsum(pair_form, query_part, key_part, preferred_element_type=jnp.float32)
        * score_scale
    )
    scores = jnp.where(allowed[:, None], scores, -jnp.inf)
    highest = jnp.max(scores, axis=-1, keepdims=True)
    weights = jnp.exp(scores - highest)
    weights = weights / jnp.sum(weights, axis=-1, keepdims=True)
    rounded = weights.astype(jnp.bfloat16)
    attended = jnp.einsum(
        "bhqk," + key_layout_shape + "->" + query_form,
        rounded,
        value_part,
        preferred_element_type=jnp.float32,
    )
    dweights = jnp.einsum(pair_form, grad_part, value_part, preferred_element_type=jnp.float32)
    delta = jnp.sum(grad_part.astype(jnp.float32) * attended, axis=-1)
    if layout == "bq":
        delta = jnp.transpose(delta, (0, 2, 1))
    else:
        delta = jnp.transpose(delta, (1, 2, 0))
    dscores = (weights * (dweights - delta[..., None]) * score_scale).astype(jnp.bfloat16)
    dquery = jnp.einsum(
        "bhqk," + key_layout_shape + "->" + query_form,
        dscores,
        key_part,
        preferred_element_type=jnp.float32,
    )
    dkey = jnp.einsum(
        "bhqk," + query_form + "->" + key_layout_shape,
        dscores,
        query_part,
        preferred_element_type=jnp.float32,
    )
    dvalue = jnp.einsum(
        "bhqk," + query_form + "->" + key_layout_shape,
        rounded,
        grad_part,
        preferred_element_type=jnp.float32,
    )
    return (attended, dquery, dkey, dvalue)


def depthwise(padded_field, taps, rows_count, cols_count, reverse_taps):
    summed = jnp.zeros((rows_count, cols_count, taps.shape[1]), jnp.float32)
    for row_offset_start in range(3):
        for offset_col in range(3):
            if reverse_taps:
                start_row = 2 - row_offset_start
                start_col = 2 - offset_col
            else:
                start_row = row_offset_start
                start_col = offset_col
            window = padded_field[
                start_row : start_row + rows_count, start_col : start_col + cols_count
            ]
            summed = summed + taps[row_offset_start * 3 + offset_col] * window.astype(jnp.float32)
    return summed


def body(query, key, value, cotangent, conv_weight, row_mask, col_mask):
    rows_here, cols_here, width = query.shape
    half_width = width // 2
    head_groups = half_width // HEAD_DIM
    row_devices = lax.axis_size("rows")
    col_devices = lax.axis_size("cols")
    sheet_rows = rows_here * row_devices
    sheet_cols = cols_here * col_devices
    taps = conv_weight.astype(jnp.float32)
    padded_value = padded(value, (("rows", 0), ("cols", 1)), 1)
    padded_grad = padded(cotangent, (("rows", 0), ("cols", 1)), 1)
    row_len = sheet_cols // SHEET_ROW_BLOCKS
    keys_row, values_row = (
        lax.all_gather(key[:, :, :half_width], "cols", axis=1, tiled=True),
        lax.all_gather(value[:, :, :half_width], "cols", axis=1, tiled=True),
    )
    col_start = lax.axis_index("cols") * cols_here
    allowed = block_allow(
        row_mask,
        col_start + jnp.arange(cols_here),
        jnp.arange(sheet_cols),
        row_len,
        SHEET_ROW_BLOCKS,
    )
    local_shape = (rows_here, cols_here, head_groups, HEAD_DIM)
    whole_shape = (rows_here, sheet_cols, head_groups, HEAD_DIM)
    results = line_attention(
        query[:, :, :half_width].reshape(local_shape),
        keys_row.reshape(whole_shape),
        values_row.reshape(whole_shape),
        cotangent[:, :, :half_width].reshape(local_shape),
        allowed,
        "bq",
    )
    key_terms = results[2].reshape(rows_here, sheet_cols, half_width)
    value_terms = results[3].reshape(rows_here, sheet_cols, half_width)
    key_grads, value_grads = (
        lax.psum_scatter(key_terms, "cols", scatter_dimension=1, tiled=True),
        lax.psum_scatter(value_terms, "cols", scatter_dimension=1, tiled=True),
    )
    out_row = results[0].reshape(rows_here, cols_here, half_width).astype(jnp.bfloat16)
    dq_row = results[1].reshape(rows_here, cols_here, half_width).astype(jnp.bfloat16)
    dk_row = key_grads.astype(jnp.bfloat16)
    dv_row = value_grads.astype(jnp.bfloat16)
    columns_each = cols_here // row_devices
    moved = (
        lax.all_to_all(query[:, :, half_width:], "rows", split_axis=1, concat_axis=0, tiled=True),
        lax.all_to_all(key[:, :, half_width:], "rows", split_axis=1, concat_axis=0, tiled=True),
        lax.all_to_all(value[:, :, half_width:], "rows", split_axis=1, concat_axis=0, tiled=True),
        lax.all_to_all(
            cotangent[:, :, half_width:], "rows", split_axis=1, concat_axis=0, tiled=True
        ),
    )
    column_shape = (sheet_rows, columns_each, head_groups, HEAD_DIM)
    my_tables = lax.dynamic_slice_in_dim(
        col_mask, lax.axis_index("rows") * columns_each, columns_each, 0
    )
    col_len = sheet_rows // COL_BLOCKS
    positions = jnp.arange(sheet_rows)
    col_allowed = block_allow(my_tables, positions, positions, col_len, COL_BLOCKS)
    col_results = line_attention(
        moved[0].reshape(column_shape),
        moved[1].reshape(column_shape),
        moved[2].reshape(column_shape),
        moved[3].reshape(column_shape),
        col_allowed,
        "qb",
    )
    column_flat = (sheet_rows, columns_each, half_width)
    col_pieces = [piece.reshape(column_flat).astype(jnp.bfloat16) for piece in col_results]
    out_col, dq_col, dk_col, dv_col = (
        lax.all_to_all(col_pieces[0], "rows", split_axis=0, concat_axis=1, tiled=True),
        lax.all_to_all(col_pieces[1], "rows", split_axis=0, concat_axis=1, tiled=True),
        lax.all_to_all(col_pieces[2], "rows", split_axis=0, concat_axis=1, tiled=True),
        lax.all_to_all(col_pieces[3], "rows", split_axis=0, concat_axis=1, tiled=True),
    )
    lepe = depthwise(padded_value, taps, rows_here, cols_here, False)
    back_conv = depthwise(padded_grad, taps, rows_here, cols_here, True)
    attended16 = jnp.concatenate([out_row, out_col], axis=2)
    out = (attended16.astype(jnp.float32) + lepe).astype(jnp.bfloat16)
    dquery = jnp.concatenate([dq_row, dq_col], axis=2)
    dkey = jnp.concatenate([dk_row, dk_col], axis=2)
    dvalue_attn = jnp.concatenate([dv_row, dv_col], axis=2)
    dvalue = (dvalue_attn.astype(jnp.float32) + back_conv).astype(jnp.bfloat16)
    return (out, dquery, dkey, dvalue)


def solution(mesh):
    return jax.shard_map(
        body,
        mesh=mesh,
        in_specs=(
            P("rows", "cols", None),
            P("rows", "cols", None),
            P("rows", "cols", None),
            P("rows", "cols", None),
            P(),
            P("rows", None, None),
            P("cols", None, None),
        ),
        out_specs=(
            P("rows", "cols", None),
            P("rows", "cols", None),
            P("rows", "cols", None),
            P("rows", "cols", None),
        ),
        check_vma=False,
    )
```

profile of v0, /device:TPU:17, one launch (start us, length us, event | category | flops | bytes accessed | tf_op | source)
XLA Modules:
  0.0 257.4 jit_solution(13641217916702605888)
XLA Ops:
  7.2 2.2 fusion.64
  13.5 17.9 %all-gather.3.cloned.1.call-done = bf16[3,256,1024]{2,1,0:T(8,128)(2,1)} async-done(((bf16[3,64,1024]{2,1,0:T(8,128)(2,1)}), bf16[3,256,1024]{2,1,0:T(8,128)(2,1)}) %all-gather.3.cloned.1.call-update) | async-done | bytes 1572880 | tf_op jit(solution)/shard_map/all_gather | solution.py:118
  31.3 1.7 copy.100
  35.4 2.1 fusion.69
  37.5 15.7 %all-gather.5.cloned.1.call-done = bf16[3,256,1024]{2,1,0:T(8,128)(2,1)} async-done(((bf16[3,64,1024]{2,1,0:T(8,128)(2,1)}), bf16[3,256,1024]{2,1,0:T(8,128)(2,1)}) %all-gather.5.cloned.1.call-update) | async-done | bytes 1572880 | tf_op jit(solution)/shard_map/all_gather | solution.py:119
  53.2 2.6 %copy.103 = bf16[3,256,1024]{1,2,0:T(8,128)(2,1)} copy(bf16[3,256,1024]{2,1,0:T(8,128)(2,1)} %all-gather.5.cloned.1.call-done) | data formatting | bytes 3145728 | tf_op jit(solution)/shard_map/all_gather | solution.py:119
  55.7 6.6 %multiply_reduce_fusion.1 = (f32[3,64,8]{1,2,0:T(8,128)}, bf16[3,8,8,8,128]{4,3,2,1,0:T(8,128)(2,1)}) fusion(bf16[3,8,8,8,128]{4,3,2,1,0:T(8,128)(2,1)} %get-tuple-element.12, bf16[3,256,8,128]{1,3,2,0:T(8,128)(2,1)} %bitcast.155, f32[3,8,64]{2,1,0:T(8,128)} %get-tuple-element.36, f32[3,8,64,256]{3,2,1,0:T(8,128)} %copy-done.3), kind=kOutput, calls=%fused_computation.64 | convolution fusion | flops 102629632 | bytes 3944448 | tf_op jit(solution)/shard_map/bhqk,bkhd->bqhd/dot_general | solution.py:54
  62.4 2.5 multiply_convert_fusion
  64.9 2.4 fusion.26
  67.2 3.5 %copy.137 = f32[3,256,1024]{2,1,0:T(8,128)} copy(f32[3,256,1024]{1,2,0:T(8,128)} %bitcast.153) | data formatting | bytes 6291456 | tf_op jit(solution)/shard_map/reshape | solution.py:139
  70.8 2.2 copy.154
  73.0 5.5 %all-to-all-start = ((bf16[3,64,1024]{2,0,1:T(4,128)(2,1)}), bf16[3,64,1024]{2,0,1:T(4,128)(2,1)}, u32[]{:S(2)}, u32[]{:S(2)}) async-start(bf16[3,64,1024]{2,0,1:T(4,128)(2,1)} %copy.154), calls=%async_computation | async-start | bytes 1048576 | tf_op jit(solution)/shard_map/all_to_all | solution.py:151
  79.6 11.3 %all-to-all-done = bf16[3,64,1024]{2,0,1:T(4,128)(2,1)} async-done(((bf16[3,64,1024]{2,0,1:T(4,128)(2,1)}), bf16[3,64,1024]{2,0,1:T(4,128)(2,1)}, u32[]{:S(2)}, u32[]{:S(2)}) %all-to-all-start) | async-done | bytes 393248 | tf_op jit(solution)/shard_map/all_to_all | solution.py:151
  90.9 5.9 %all-to-all-start.1 = ((bf16[3,64,1024]{2,0,1:T(4,128)(2,1)}), bf16[3,64,1024]{2,0,1:T(4,128)(2,1)}, u32[]{:S(2)}, u32[]{:S(2)}) async-start(bf16[3,64,1024]{2,0,1:T(4,128)(2,1)} %copy.155), calls=%async_computation.1 | async-start | bytes 1048576 | tf_op jit(solution)/shard_map/all_to_all | solution.py:152
  97.7 3.1 %collective-permute-start.1 = (bf16[1,64,2048]{2,1,0:T(8,128)(2,1)}, bf16[1,64,2048]{2,1,0:T(8,128)(2,1)}, u32[]{:S(2)}, u32[]{:S(2)}) collective-permute-start(bf16[1,64,2048]{2,1,0:T(8,128)(2,1)} %get-tuple-element.22), channel_id=1, source_target_pairs={{4,0},{8,4},{12,8},{16,12},{20,16},{24,20},{28,24},{5,1},{9,5},{13... | collective-permute-start | bytes 786440 | tf_op jit(solution)/shard_map/ppermute | solution.py:21
  100.8 2.2 collective-permute-start
  103.0 2.2 copy.156
  105.1 3.7 %all-to-all-done.1 = bf16[3,64,1024]{2,0,1:T(4,128)(2,1)} async-done(((bf16[3,64,1024]{2,0,1:T(4,128)(2,1)}), bf16[3,64,1024]{2,0,1:T(4,128)(2,1)}, u32[]{:S(2)}, u32[]{:S(2)}) %all-to-all-start.1) | async-done | bytes 393248 | tf_op jit(solution)/shard_map/all_to_all | solution.py:152
  108.9 6.3 %all-to-all-start.2 = ((bf16[3,64,1024]{2,0,1:T(4,128)(2,1)}), bf16[3,64,1024]{2,0,1:T(4,128)(2,1)}, u32[]{:S(2)}, u32[]{:S(2)}) async-start(bf16[3,64,1024]{2,0,1:T(4,128)(2,1)} %copy.156), calls=%async_computation.2 | async-start | bytes 1048576 | tf_op jit(solution)/shard_map/all_to_all | solution.py:153
  116.0 3.1 %collective-permute-start.5 = (bf16[1,64,2048]{2,1,0:T(8,128)(2,1)}, bf16[1,64,2048]{2,1,0:T(8,128)(2,1)}, u32[]{:S(2)}, u32[]{:S(2)}) collective-permute-start(bf16[1,64,2048]{2,1,0:T(8,128)(2,1)} %get-tuple-element.8), channel_id=1, source_target_pairs={{4,0},{8,4},{12,8},{16,12},{20,16},{24,20},{28,24},{5,1},{9,5},{13... | collective-permute-start | bytes 786440 | tf_op jit(solution)/shard_map/ppermute | solution.py:21
  119.1 2.2 collective-permute-start.4
  125.7 6.6 %all-to-all-start.4 = ((bf16[3,64,1024]{2,0,1:T(4,128)(2,1)}), bf16[3,64,1024]{2,0,1:T(4,128)(2,1)}, u32[]{:S(2)}, u32[]{:S(2)}) async-start(bf16[3,64,1024]{2,0,1:T(4,128)(2,1)} %copy.157), calls=%async_computation.4 | async-start | bytes 1048576 | tf_op jit(solution)/shard_map/all_to_all | solution.py:154
  132.3 6.8 %fusion.23 = f32[3,8,256,128]{2,3,1,0:T(8,128)} fusion(bf16[3,8,8,8,128]{4,3,2,1,0:T(8,128)(2,1)} %get-tuple-element.12, f32[3,8,64]{2,1,0:T(8,128)} %get-tuple-element.36, f32[3,8,64,256]{3,2,1,0:T(8,128)} %copy-done.3), kind=kOutput, calls=%fused_computation.73 | convolution fusion | flops 101844736 | bytes 5117952 | tf_op jit(solution)/shard_map/bhqk,bqhd->bkhd/dot_general | solution.py:79
  139.0 3.6 %copy.142 = f32[3,256,1024]{2,1,0:T(8,128)} copy(f32[3,256,1024]{1,2,0:T(8,128)} %bitcast.154) | data formatting | bytes 6291456 | tf_op jit(solution)/shard_map/reshape | solution.py:140
  144.1 1.9 copy.110
  146.1 1.9 copy.112
  152.4 1.7 fusion.68
  155.2 3.3 %fusion.12 = bf16[24,8,8,128]{3,0,2,1:T(8,128)(2,1)} fusion(bf16[24,8,8,128]{3,2,1,0:T(8,128)(2,1)} %get-tuple-element.40, f32[8,8,24]{2,1,0:T(8,128)} %get-tuple-element.33, f32[8,8,24,24]{2,3,1,0:T(8,128)} %copy-done.17), kind=kOutput, calls=%fused_computation.40 | convolution fusion | flops 9745943 | bytes 940032 | tf_op jit(solution)/shard_map/bhqk,qbhd->kbhd/dot_general | solution.py:79
  160.6 5.4 %all-to-all-start.7 = ((bf16[24,8,1024]{2,1,0:T(8,128)(2,1)}), bf16[24,8,1024]{2,1,0:T(8,128)(2,1)S(1)}, u32[]{:S(2)}, u32[]{:S(2)}) async-start(bf16[24,8,1024]{2,1,0:T(8,128)(2,1)} %convert_element_type.188), calls=%async_computation.9 | async-start | bytes 786432 | tf_op jit(solution)/shard_map/all_to_all | solution.py:179
  166.0 3.7 %multiply_reduce_fusion = (f32[24,8,8]{0,2,1:T(8,128)}, bf16[24,8,8,128]{3,0,2,1:T(8,128)(2,1)}) fusion(bf16[24,8,8,128]{3,2,1,0:T(8,128)(2,1)} %get-tuple-element.40, bf16[24,8,8,128]{3,2,1,0:T(8,128)(2,1)} %get-tuple-element.41, f32[8,8,24]{2,1,0:T(8,128)} %get-tuple-element.33, f32[8,8,24,24]{2,3,1,0:T(8,128)} %copy-done.17), kind=kOutput, calls=%fused_computation.63 | convolution fusion | flops 10334231 | bytes 1339392 | tf_op jit(solution)/shard_map/bhqk,kbhd->qbhd/dot_general | solution.py:54
  169.7 2.1 fusion.9
  173.4 1.9 convert_element_type.184
  175.4 5.5 %all-to-all-start.6 = ((bf16[24,8,1024]{2,1,0:T(8,128)(2,1)}), bf16[24,8,1024]{2,1,0:T(8,128)(2,1)}, u32[]{:S(2)}, u32[]{:S(2)}) async-start(bf16[24,8,1024]{2,1,0:T(8,128)(2,1)} %convert_element_type.184), calls=%async_computation.7 | async-start | bytes 786432 | tf_op jit(solution)/shard_map/all_to_all | solution.py:178
  180.8 1.8 constant_dynamic-update-slice_fusion.5
  184.8 1.9 convert_element_type.180
  187.0 6.0 %all-to-all-start.5 = ((bf16[24,8,1024]{2,1,0:T(8,128)(2,1)}), bf16[24,8,1024]{2,1,0:T(8,128)(2,1)}, u32[]{:S(2)}, u32[]{:S(2)}) async-start(bf16[24,8,1024]{2,1,0:T(8,128)(2,1)} %convert_element_type.180), calls=%async_computation.5 | async-start | bytes 786432 | tf_op jit(solution)/shard_map/all_to_all | solution.py:177
  194.6 1.7 fusion.61
  196.3 9.2 %collective-permute-start.6 = (bf16[5,1,2048]{2,1,0:T(2,128)(2,1)}, bf16[5,1,2048]{2,1,0:T(2,128)(2,1)}, u32[]{:S(2)}, u32[]{:S(2)}) collective-permute-start(bf16[5,1,2048]{2,1,0:T(2,128)(2,1)} %get-tuple-element.4), channel_id=1, source_target_pairs={{1,0},{2,1},{3,2},{5,4},{6,5},{7,6},{9,8},{10,9},{11,10},{13,12},{... | collective-permute-start | bytes 61448 | tf_op jit(solution)/shard_map/ppermute | solution.py:21
  205.5 2.0 collective-permute-start.7
  209.2 1.8 copy.119
  211.0 1.9 convert_element_type.158
  212.9 5.5 %all-to-all-start.3 = ((bf16[24,8,1024]{2,1,0:T(8,128)(2,1)}), bf16[24,8,1024]{2,1,0:T(8,128)(2,1)}, u32[]{:S(2)}, u32[]{:S(2)}) async-start(bf16[24,8,1024]{2,1,0:T(8,128)(2,1)} %convert_element_type.158), calls=%async_computation.3 | async-start | bytes 786432 | tf_op jit(solution)/shard_map/all_to_all | solution.py:176
  222.7 3.5 %collective-permute-start.2 = (bf16[5,1,2048]{2,1,0:T(2,128)(2,1)}, bf16[5,1,2048]{2,1,0:T(2,128)(2,1)}, u32[]{:S(2)}, u32[]{:S(2)}) collective-permute-start(bf16[5,1,2048]{2,1,0:T(2,128)(2,1)} %get-tuple-element.6), channel_id=1, source_target_pairs={{0,1},{1,2},{2,3},{4,5},{5,6},{6,7},{8,9},{9,10},{10,11},{12,13},{... | collective-permute-start | bytes 61448 | tf_op jit(solution)/shard_map/ppermute | solution.py:20
  226.3 2.1 collective-permute-start.3
  230.2 1.8 copy.220
  233.0 1.9 fusion.13
  236.7 4.8 %add_convert_fusion.1 = bf16[3,64,2048]{2,1,0:T(8,128)(2,1)} fusion(bf16[3,64,2048]{2,1,0:T(8,128)(2,1)S(1)} %copy-done.1, bf16[5,64,2048]{2,1,0:T(8,128)(2,1)S(1)} %copy-done.5, bf16[5,1,2048]{2,1,0:T(2,128)(2,1)} %collective-permute-done.3, bf16[5,1,2048]{2,1,0:T(2,128)(2,1)} %collective-permute-done.2, bf16[1,64,2048]{2,1,0:T(8,128)(2,1)} %collective-permute-done.1, ...), kind=kLoop, calls=%fused_computation.13 | loop fusion | flops 22020096 | bytes 4308992 | tf_op jit(solution)/shard_map/convert_element_type | solution.py:184
  244.8 6.1 %add_convert_fusion = bf16[3,64,2048]{2,1,0:T(8,128)(2,1)} fusion(bf16[3,64,2048]{2,1,0:T(8,128)(2,1)S(1)} %copy-done.2, bf16[5,64,2048]{2,1,0:T(8,128)(2,1)} %constant_dynamic-update-slice_fusion.3, bf16[5,1,2048]{2,1,0:T(2,128)(2,1)} %collective-permute-done.7, bf16[5,1,2048]{2,1,0:T(2,128)(2,1)} %collective-permute-done.6, ...), kind=kLoop, calls=%fused_computation.11 | loop fusion | flops 22020096 | bytes 4308992 | tf_op jit(solution)/shard_map/convert_element_type | solution.py:188
  (129 shorter events, 42.1 us)
Async XLA Ops:
  7.2 114.1 %copy-start = (s32[64,3,3]{0,2,1:T(4,128)S(1)}, s32[64,3,3]{0,2,1:T(4,128)}, u32[]{:S(2)}) copy-start(s32[64,3,3]{0,2,1:T(4,128)} %param.13) | copy-start | bytes 6916
  7.2 2.3 copy-start.1
  7.2 24.1 %all-gather.3.cloned.1.call-start = ((), (), s32[]{:S(2)}) async-start(), calls=%async_computation.10 | async-start | bytes 1966080 | tf_op jit(solution)/shard_map/all_gather | solution.py:118
  9.4 1.1 copy-start.29
  9.4 2.3 copy-start.16
  9.4 3.1 %copy-start.2 = (bf16[3,64,2048]{2,1,0:T(8,128)(2,1)S(1)}, bf16[3,64,2048]{2,1,0:T(8,128)(2,1)}, u32[]{:S(2)}) copy-start(bf16[3,64,2048]{2,1,0:T(8,128)(2,1)} %param.10) | copy-start | bytes 2359300
  9.4 43.7 %all-gather.5.cloned.1.call-start = ((), (), s32[]{:S(2)}) async-start(), calls=%async_computation.11 | async-start | bytes 1966080 | tf_op jit(solution)/shard_map/all_gather | solution.py:119
  10.5 231.0 %reduce-scatter.3.cloned.1.call-start = ((), (), s32[]{:S(2)}) async-start(), calls=%async_computation.12 | async-start | bytes 3932160 | tf_op jit(solution)/shard_map/reduce_scatter | solution.py:142
  34.2 1.2 copy-start.3
  64.9 2.4 copy-start.4
  70.8 7.7 %copy-start.7 = (bf16[3,64,1024]{2,1,0:T(8,128)(2,1)S(1)}, bf16[3,64,1024]{2,1,0:T(8,128)(2,1)}, u32[]{:S(2)}) copy-start(bf16[3,64,1024]{2,1,0:T(8,128)(2,1)} %get-tuple-element.19) | copy-start | bytes 1179652
  73.0 17.9 %all-to-all-start = ((bf16[3,64,1024]{2,0,1:T(4,128)(2,1)}), bf16[3,64,1024]{2,0,1:T(4,128)(2,1)}, u32[]{:S(2)}, u32[]{:S(2)}) async-start(bf16[3,64,1024]{2,0,1:T(4,128)(2,1)} %copy.154), calls=%async_computation | async-start | bytes 1048576 | tf_op jit(solution)/shard_map/all_to_all | solution.py:151
  90.9 17.9 %all-to-all-start.1 = ((bf16[3,64,1024]{2,0,1:T(4,128)(2,1)}), bf16[3,64,1024]{2,0,1:T(4,128)(2,1)}, u32[]{:S(2)}, u32[]{:S(2)}) async-start(bf16[3,64,1024]{2,0,1:T(4,128)(2,1)} %copy.155), calls=%async_computation.1 | async-start | bytes 1048576 | tf_op jit(solution)/shard_map/all_to_all | solution.py:152
  97.7 121.7 %collective-permute-start.1 = (bf16[1,64,2048]{2,1,0:T(8,128)(2,1)}, bf16[1,64,2048]{2,1,0:T(8,128)(2,1)}, u32[]{:S(2)}, u32[]{:S(2)}) collective-permute-start(bf16[1,64,2048]{2,1,0:T(8,128)(2,1)} %get-tuple-element.22), channel_id=1, source_target_pairs={{4,0},{8,4},{12,8},{16,12},{20,16},{24,20},{28,24},{5,1},{9,5},{13... | collective-permute-start | bytes 786440 | tf_op jit(solution)/shard_map/ppermute | solution.py:21
  100.8 106.7 %collective-permute-start = (bf16[1,64,2048]{2,1,0:T(8,128)(2,1)}, bf16[1,64,2048]{2,1,0:T(8,128)(2,1)}, u32[]{:S(2)}, u32[]{:S(2)}) collective-permute-start(bf16[1,64,2048]{2,1,0:T(8,128)(2,1)} %get-tuple-element.23), channel_id=1, source_target_pairs={{0,4},{4,8},{8,12},{12,16},{16,20},{20,24},{24,28},{1,5},{5,9},{9,... | collective-permute-start | bytes 786440 | tf_op jit(solution)/shard_map/ppermute | solution.py:20
  103.0 20.9 %copy-start.6 = (bf16[3,64,1024]{2,1,0:T(8,128)(2,1)S(1)}, bf16[3,64,1024]{2,1,0:T(8,128)(2,1)}, u32[]{:S(2)}) copy-start(bf16[3,64,1024]{2,1,0:T(8,128)(2,1)} %get-tuple-element.13) | copy-start | bytes 1179652
  108.9 16.8 %all-to-all-start.2 = ((bf16[3,64,1024]{2,0,1:T(4,128)(2,1)}), bf16[3,64,1024]{2,0,1:T(4,128)(2,1)}, u32[]{:S(2)}, u32[]{:S(2)}) async-start(bf16[3,64,1024]{2,0,1:T(4,128)(2,1)} %copy.156), calls=%async_computation.2 | async-start | bytes 1048576 | tf_op jit(solution)/shard_map/all_to_all | solution.py:153
  116.0 77.0 %collective-permute-start.5 = (bf16[1,64,2048]{2,1,0:T(8,128)(2,1)}, bf16[1,64,2048]{2,1,0:T(8,128)(2,1)}, u32[]{:S(2)}, u32[]{:S(2)}) collective-permute-start(bf16[1,64,2048]{2,1,0:T(8,128)(2,1)} %get-tuple-element.8), channel_id=1, source_target_pairs={{4,0},{8,4},{12,8},{16,12},{20,16},{24,20},{28,24},{5,1},{9,5},{13... | collective-permute-start | bytes 786440 | tf_op jit(solution)/shard_map/ppermute | solution.py:21
  119.1 61.8 %collective-permute-start.4 = (bf16[1,64,2048]{2,1,0:T(8,128)(2,1)}, bf16[1,64,2048]{2,1,0:T(8,128)(2,1)}, u32[]{:S(2)}, u32[]{:S(2)}) collective-permute-start(bf16[1,64,2048]{2,1,0:T(8,128)(2,1)} %get-tuple-element.9), channel_id=1, source_target_pairs={{0,4},{4,8},{8,12},{12,16},{16,20},{20,24},{24,28},{1,5},{5,9},{9,... | collective-permute-start | bytes 786440 | tf_op jit(solution)/shard_map/ppermute | solution.py:20
  125.7 23.5 %all-to-all-start.4 = ((bf16[3,64,1024]{2,0,1:T(4,128)(2,1)}), bf16[3,64,1024]{2,0,1:T(4,128)(2,1)}, u32[]{:S(2)}, u32[]{:S(2)}) async-start(bf16[3,64,1024]{2,0,1:T(4,128)(2,1)} %copy.157), calls=%async_computation.4 | async-start | bytes 1048576 | tf_op jit(solution)/shard_map/all_to_all | solution.py:154
  132.3 111.3 %reduce-scatter.5.cloned.1.call-start = ((), (), s32[]{:S(2)}) async-start(), calls=%async_computation.13 | async-start | bytes 3932160 | tf_op jit(solution)/shard_map/reduce_scatter | solution.py:143
  149.2 2.5 copy-start.28
  151.7 2.4 copy-start.10
  151.8 2.4 copy-start.12
  152.4 2.8 %copy-start.17 = (f32[8,8,24,24]{2,3,1,0:T(8,128)}, f32[8,8,24,24]{2,3,1,0:T(8,128)S(1)}, u32[]{:S(2)}) copy-start(f32[8,8,24,24]{2,3,1,0:T(8,128)S(1)} %fusion.6) | copy-start | bytes 442372
  160.6 14.8 %all-to-all-start.7 = ((bf16[24,8,1024]{2,1,0:T(8,128)(2,1)}), bf16[24,8,1024]{2,1,0:T(8,128)(2,1)S(1)}, u32[]{:S(2)}, u32[]{:S(2)}) async-start(bf16[24,8,1024]{2,1,0:T(8,128)(2,1)} %convert_element_type.188), calls=%async_computation.9 | async-start | bytes 786432 | tf_op jit(solution)/shard_map/all_to_all | solution.py:179
  169.7 2.1 copy-start.13
  175.4 11.6 %all-to-all-start.6 = ((bf16[24,8,1024]{2,1,0:T(8,128)(2,1)}), bf16[24,8,1024]{2,1,0:T(8,128)(2,1)}, u32[]{:S(2)}, u32[]{:S(2)}) async-start(bf16[24,8,1024]{2,1,0:T(8,128)(2,1)} %convert_element_type.184), calls=%async_computation.7 | async-start | bytes 786432 | tf_op jit(solution)/shard_map/all_to_all | solution.py:178
  180.8 2.7 %copy-start.11 = (bf16[24,8,8,128]{3,2,1,0:T(8,128)(2,1)S(1)}, bf16[24,8,8,128]{3,2,1,0:T(8,128)(2,1)}, u32[]{:S(2)}) copy-start(bf16[24,8,8,128]{3,2,1,0:T(8,128)(2,1)} %copy-done.10) | copy-start | bytes 1179652
  180.8 2.7 %copy-start.15 = (bf16[8,8,24,24]{2,3,1,0:T(8,128)(2,1)S(1)}, bf16[8,8,24,24]{2,3,1,0:T(8,128)(2,1)}, u32[]{:S(2)}) copy-start(bf16[8,8,24,24]{2,3,1,0:T(8,128)(2,1)} %copy-done.14) | copy-start | bytes 221188
  187.0 25.9 %all-to-all-start.5 = ((bf16[24,8,1024]{2,1,0:T(8,128)(2,1)}), bf16[24,8,1024]{2,1,0:T(8,128)(2,1)}, u32[]{:S(2)}, u32[]{:S(2)}) async-start(bf16[24,8,1024]{2,1,0:T(8,128)(2,1)} %convert_element_type.180), calls=%async_computation.5 | async-start | bytes 786432 | tf_op jit(solution)/shard_map/all_to_all | solution.py:177
  196.3 48.5 %collective-permute-start.6 = (bf16[5,1,2048]{2,1,0:T(2,128)(2,1)}, bf16[5,1,2048]{2,1,0:T(2,128)(2,1)}, u32[]{:S(2)}, u32[]{:S(2)}) collective-permute-start(bf16[5,1,2048]{2,1,0:T(2,128)(2,1)} %get-tuple-element.4), channel_id=1, source_target_pairs={{1,0},{2,1},{3,2},{5,4},{6,5},{7,6},{9,8},{10,9},{11,10},{13,12},{... | collective-permute-start | bytes 61448 | tf_op jit(solution)/shard_map/ppermute | solution.py:21
  205.5 39.3 %collective-permute-start.7 = (bf16[5,1,2048]{2,1,0:T(2,128)(2,1)}, bf16[5,1,2048]{2,1,0:T(2,128)(2,1)}, u32[]{:S(2)}, u32[]{:S(2)}) collective-permute-start(bf16[5,1,2048]{2,1,0:T(2,128)(2,1)} %get-tuple-element.5), channel_id=1, source_target_pairs={{0,1},{1,2},{2,3},{4,5},{5,6},{6,7},{8,9},{9,10},{10,11},{12,13},{... | collective-permute-start | bytes 61448 | tf_op jit(solution)/shard_map/ppermute | solution.py:20
  212.9 19.1 %all-to-all-start.3 = ((bf16[24,8,1024]{2,1,0:T(8,128)(2,1)}), bf16[24,8,1024]{2,1,0:T(8,128)(2,1)}, u32[]{:S(2)}, u32[]{:S(2)}) async-start(bf16[24,8,1024]{2,1,0:T(8,128)(2,1)} %convert_element_type.158), calls=%async_computation.3 | async-start | bytes 786432 | tf_op jit(solution)/shard_map/all_to_all | solution.py:176
  222.7 13.5 %collective-permute-start.2 = (bf16[5,1,2048]{2,1,0:T(2,128)(2,1)}, bf16[5,1,2048]{2,1,0:T(2,128)(2,1)}, u32[]{:S(2)}, u32[]{:S(2)}) collective-permute-start(bf16[5,1,2048]{2,1,0:T(2,128)(2,1)} %get-tuple-element.6), channel_id=1, source_target_pairs={{0,1},{1,2},{2,3},{4,5},{5,6},{6,7},{8,9},{9,10},{10,11},{12,13},{... | collective-permute-start | bytes 61448 | tf_op jit(solution)/shard_map/ppermute | solution.py:20
  226.3 9.9 %collective-permute-start.3 = (bf16[5,1,2048]{2,1,0:T(2,128)(2,1)}, bf16[5,1,2048]{2,1,0:T(2,128)(2,1)}, u32[]{:S(2)}, u32[]{:S(2)}) collective-permute-start(bf16[5,1,2048]{2,1,0:T(2,128)(2,1)} %get-tuple-element.7), channel_id=1, source_target_pairs={{1,0},{2,1},{3,2},{5,4},{6,5},{7,6},{9,8},{10,9},{11,10},{13,12},{... | collective-permute-start | bytes 61448 | tf_op jit(solution)/shard_map/ppermute | solution.py:21
  233.0 2.1 copy-start.9
  234.9 1.2 copy-start.18
  234.9 1.7 copy-start.5
  234.9 1.7 copy-start.20
  234.9 1.7 copy-start.21
  234.9 1.7 copy-start.22
  234.9 1.7 copy-start.23
  234.9 1.7 copy-start.24
  234.9 1.7 copy-start.25
  235.0 1.7 copy-start.26
  235.0 1.7 copy-start.27
  242.6 2.2 copy-start.8
  (2 other events, 1.6 us)
Sparse Core Ops, SparseCore 0:
  10.2 21.1 all-gather.2
  33.5 19.6 all-gather.4
  70.9 37.5 reduce-scatter.2
  142.8 42.4 reduce-scatter.4
where the time goes:
time: 260 us; the launch traced here: 257 us
  starting transfers between devices  74.1 us (28%)
  local copies, waits for them, and re-layouts  66.4 us (26%)
  waiting for transfers between devices  49.7 us (19%)
  matrix products  34 us (13%)
  other arithmetic  18.9 us (7%)
  between operations  14.3 us (6%)
    all_gather x1, waiting for transfers between devices, body(): lax.all_gather(key[:, :, :half_width], 'cols', axis=1, tiled=True)  17.9 us
    ppermute x4, starting transfers between devices, padded(): after = lax.ppermute(leading, axis, down)  17.5 us
    unnamed x70, local copies, waits for them, and re-layouts  16.6 us
    all_gather x1, waiting for transfers between devices, body(): lax.all_gather(value[:, :, :half_width], 'cols', axis=1, tiled=True)  15.7 us
    all_to_all x1, waiting for transfers between devices, body(): lax.all_to_all(query[:, :, half_width:], 'rows', split_axis=1, concat_axi...  11.3 us
    convert_element_type x8, local copies, waits for them, and re-layouts, body(): piece.reshape(column_flat).astype(jnp.bfloat16)  11.3 us
    dot_general x2, matrix products, line_attention(): jnp.einsum('bhqk,' + key_layout_shape + '->' + query_form, rounded, value...  10.4 us
    dot_general x2, matrix products, line_attention(): jnp.einsum('bhqk,' + query_form + '->' + key_layout_shape, rounded, grad_...  10.1 us
  transfers between devices with their start and end apart: 20, of which 6 were waited for; matrix products, arithmetic and copies ran while one was open for 35% of the time, Pallas kernels for 0%

commit v1 on v0

--- a/solution.py
+++ b/solution.py
@@ -1,8 +1,11 @@
+import functools
 import math
 
 import jax
 import jax.numpy as jnp
 from jax import lax
+from jax.experimental import pallas as pl
+from jax.experimental.pallas import tpu as pltpu
 from jax.sharding import PartitionSpec as P
 
 HEAD_DIM = 128
@@ -189,9 +192,336 @@
     return (out, dquery, dkey, dvalue)
 
 
+SUB = 8
+CHUNKS = 2
+MESH = pl.DeviceIdType.MESH
+
+
+def attend(q, k, v, g, allow):
+    scale = 1.0 / math.sqrt(HEAD_DIM)
+    nt = (((1,), (1,)), ((), ()))
+    nn = (((1,), (0,)), ((), ()))
+    tn = (((0,), (0,)), ((), ()))
+    dot = functools.partial(lax.dot_general, preferred_element_type=jnp.float32)
+    s = jnp.where(allow, dot(q, k, nt) * scale, -jnp.inf)
+    e = jnp.exp(s - jnp.max(s, axis=-1, keepdims=True))
+    w = e * (1.0 / jnp.sum(e, axis=-1, keepdims=True))
+    w16 = w.astype(jnp.bfloat16)
+    att = dot(w16, v, nn)
+    dw = dot(g, v, nt)
+    delta = jnp.sum(g.astype(jnp.float32) * att, axis=-1, keepdims=True)
+    ds = (w * (dw - delta) * scale).astype(jnp.bfloat16)
+    return att, dot(ds, k, nn), dot(ds, q, tn), dot(w16, g, tn)
+
+
+def layer_kernel(
+    dims, q_hbm, k_hbm, v_hbm, g_hbm, taps, row_allow, col_allow, *rest
+):
+    R, C, rows, groups, width = dims
+    outs_hbm = rest[:4]
+    colbuf, colout, rowbuf, rowout, ext, conv, ret, done = rest[4:12]
+    (ci_s, ci_r, co_s, co_r, ri_s, ri_r, ro_s, ro_r, ha_s, ha_r, local, final) = rest[12:]
+    half = width // 2
+    share = half // C
+    part = half // CHUNKS
+    me = lax.axis_index("rows")
+    mc = lax.axis_index("cols")
+    inputs = (q_hbm, k_hbm, v_hbm, g_hbm)
+    f32 = jnp.float32
+
+    def lanes(start, size):
+        return pl.ds(pl.multiple_of(start, 128), size)
+
+    def col_in(t, ch, p, slot):
+        return pltpu.make_async_remote_copy(
+            src_ref=inputs[t].at[:, p, :, pl.ds(half + ch * part, part)],
+            dst_ref=colbuf.at[t, slot, :, :, pl.ds(ch * part, part)],
+            send_sem=ci_s.at[t, ch, p], recv_sem=ci_r.at[t, ch, slot],
+            device_id={"rows": p}, device_id_type=MESH)
+
+    def col_back(t, ch, p, slot):
+        return pltpu.make_async_remote_copy(
+            src_ref=colout.at[t, p, :, :, pl.ds(ch * part, part)],
+            dst_ref=ret.at[t, :, slot, :, pl.ds(half + ch * part, part)],
+            send_sem=co_s.at[t, ch, p], recv_sem=co_r.at[t, ch, slot],
+            device_id={"rows": p}, device_id_type=MESH)
+
+    def row_in(t, p, slot):
+        return pltpu.make_async_remote_copy(
+            src_ref=inputs[t].at[:, :, :, lanes(p * share, share)],
+            dst_ref=rowbuf.at[t, :, slot],
+            send_sem=ri_s.at[t, p], recv_sem=ri_r.at[t, slot],
+            device_id={"cols": p}, device_id_type=MESH)
+
+    def row_back(t, p, slot):
+        return pltpu.make_async_remote_copy(
+            src_ref=rowout.at[t, :, p],
+            dst_ref=ret.at[t, :, :, :, lanes(slot * share, share)],
+            send_sem=ro_s.at[t, p], recv_sem=ro_r.at[t, slot],
+            device_id={"cols": p}, device_id_type=MESH)
+
+    def row_span(dr, there):
+        if dr == 0:
+            return pl.ds(1, rows) if there else pl.ds(0, rows)
+        if dr == 1:
+            return pl.ds(0, 1) if there else pl.ds(rows - 1, 1)
+        return pl.ds(rows + 1, 1) if there else pl.ds(0, 1)
+
+    def group_span(dc, there):
+        if dc == 0:
+            return pl.ds(1, groups) if there else pl.ds(0, groups)
+        if dc == 1:
+            return pl.ds(0, 1) if there else pl.ds(groups - 1, 1)
+        return pl.ds(groups + 1, 1) if there else pl.ds(0, 1)
+
+    directions = [(a, b) for a in (-1, 0, 1) for b in (-1, 0, 1) if (a, b) != (0, 0)]
+
+    def halo(t, i):
+        dr, dc = directions[i]
+        return pltpu.make_async_remote_copy(
+            src_ref=inputs[2 + t].at[row_span(dr, False), group_span(dc, False)],
+            dst_ref=ext.at[t, row_span(dr, True), group_span(dc, True)],
+            send_sem=ha_s.at[t, i], recv_sem=ha_r.at[t, i],
+            device_id={"rows": me + dr, "cols": mc + dc}, device_id_type=MESH)
+
+    def has(i, sign):
+        dr, dc = directions[i]
+        conds = []
+        if sign * dr == 1:
+            conds.append(me < R - 1)
+        if sign * dr == -1:
+            conds.append(me > 0)
+        if sign * dc == 1:
+            conds.append(mc < C - 1)
+        if sign * dc == -1:
+            conds.append(mc > 0)
+        ok = conds[0]
+        for c in conds[1:]:
+            ok = jnp.logical_and(ok, c)
+        return ok
+
+    barrier = pltpu.get_barrier_semaphore()
+    for d in range(1, R):
+        pl.semaphore_signal(barrier, inc=1, device_id={"rows": lax.rem(me + d, R)}, device_id_type=MESH)
+    for d in range(1, C):
+        pl.semaphore_signal(barrier, inc=1, device_id={"cols": lax.rem(mc + d, C)}, device_id_type=MESH)
+    for dr, dc in ((1, 1), (1, -1), (-1, 1), (-1, -1)):
+        corner = {"rows": lax.rem(me + dr + R, R), "cols": lax.rem(mc + dc + C, C)}
+        pl.semaphore_signal(barrier, inc=1, device_id=corner, device_id_type=MESH)
+    pl.semaphore_wait(barrier, R - 1 + C - 1 + 4)
+
+    order = sorted(range(1, R), key=lambda d: abs(d - R / 2))
+    col_order = sorted(range(1, C), key=lambda d: abs(d - C / 2))
+    for d in col_order:
+        for t in range(4):
+            row_in(t, lax.rem(mc + d, C), mc).start()
+    for ch in range(CHUNKS):
+        for d in order:
+            for t in range(4):
+                col_in(t, ch, lax.rem(me + d, R), me).start()
+    for t in range(2):
+        for i in range(8):
+            @pl.when(has(i, 1))
+            def _(t=t, i=i):
+                halo(t, i).start()
+
+    mine = []
+    for t in range(4):
+        mine.append(pltpu.make_async_copy(inputs[t].at[:, :, :, lanes(mc * share, share)], rowbuf.at[t, :, mc], local.at[0, t]))
+        mine.append(pltpu.make_async_copy(inputs[t].at[:, me, :, pl.ds(half, half)], colbuf.at[t, me], local.at[1, t]))
+    for t in range(2):
+        mine.append(pltpu.make_async_copy(inputs[2 + t], ext.at[t, pl.ds(1, rows), pl.ds(1, groups)], local.at[2, t]))
+    for c in mine:
+        c.start()
+    for t in range(2):
+        for i in range(8):
+            @pl.when(jnp.logical_not(has(i, -1)))
+            def _(t=t, i=i):
+                dr, dc = directions[i]
+                view = ext.at[t, row_span(dr, True), group_span(dc, True)]
+                view[...] = jnp.zeros(view.shape, view.dtype)
+    for c in mine:
+        c.wait()
+
+    for d in col_order:
+        for t in range(4):
+            p = lax.rem(mc + d, C)
+            row_in(t, p, p).wait_recv()
+    tokens = C * groups * SUB
+
+    def row_step(n, carry):
+        i, h = n // (share // HEAD_DIM), lax.rem(n, share // HEAD_DIM)
+        cols = lanes(h * HEAD_DIM, HEAD_DIM)
+        x = [rowbuf[t, i, :, :, :, cols].astype(f32).reshape(tokens, HEAD_DIM).astype(jnp.bfloat16) for t in range(4)]
+        table = row_allow[i]
+        size = tokens // SHEET_ROW_BLOCKS
+        allow = jnp.concatenate(
+            [jnp.broadcast_to(table[b : b + 1], (size, tokens)) for b in range(SHEET_ROW_BLOCKS)], axis=0) > 0.5
+        for t, y in enumerate(attend(*x, allow)):
+            rowout[t, i, :, :, :, cols] = y.reshape(C, groups, SUB, HEAD_DIM).astype(jnp.bfloat16)
+        return carry
+
+    lax.fori_loop(0, rows * (share // HEAD_DIM), row_step, 0)
+    for d in col_order:
+        for t in range(4):
+            row_back(t, lax.rem(mc + d, C), mc).start()
+    mine = [pltpu.make_async_copy(rowout.at[t, :, mc], ret.at[t, :, :, :, lanes(mc * share, share)], local.at[0, t]) for t in range(4)]
+    for c in mine:
+        c.start()
+
+    length = R * rows * SUB
+    col_size = length // COL_BLOCKS
+    for ch in range(CHUNKS):
+        for d in order:
+            for t in range(4):
+                p = lax.rem(me + d, R)
+                col_in(t, ch, p, p).wait_recv()
+        allow = jnp.concatenate(
+            [jnp.broadcast_to(col_allow[b][None], (col_size // SUB, SUB, length)).reshape(col_size, length) for b in range(COL_BLOCKS)], axis=0) > 0.5
+
+        def col_step(h, carry):
+            cols = lanes(ch * part + h * HEAD_DIM, HEAD_DIM)
+            x = [colbuf[t, :, :, :, cols].astype(f32).reshape(length, HEAD_DIM).astype(jnp.bfloat16) for t in range(4)]
+            for t, y in enumerate(attend(*x, allow)):
+                colout[t, :, :, :, cols] = y.reshape(R, rows, SUB, HEAD_DIM).astype(jnp.bfloat16)
+            return carry
+
+        lax.fori_loop(0, part // HEAD_DIM, col_step, 0)
+        for d in order:
+            for t in range(4):
+                col_back(t, ch, lax.rem(me + d, R), me).start()
+    own = [pltpu.make_async_copy(colout.at[t, me], ret.at[t, :, me, :, pl.ds(half, half)], local.at[1, t]) for t in range(4)]
+    for c in own:
+        c.start()
+
+    for t in range(2):
+        for i in range(8):
+            @pl.when(has(i, -1))
+            def _(t=t, i=i):
+                pltpu.make_async_remote_copy(
+                    src_ref=inputs[2 + t].at[row_span(directions[i][0], False), group_span(directions[i][1], False)],
+                    dst_ref=ext.at[t, row_span(directions[i][0], True), group_span(directions[i][1], True)],
+                    send_sem=ha_s.at[t, i], recv_sem=ha_r.at[t, i],
+                    device_id={"rows": me - directions[i][0], "cols": mc - directions[i][1]}, device_id_type=MESH).wait_recv()
+    long = groups * SUB
+
+    def conv_step(n, carry):
+        cols = lanes(n * 128, 128)
+        weights = taps[:, cols].astype(f32)
+        for t in range(2):
+            sums = [None] * rows
+            for r in range(rows + 2):
+                line = ext[t, r, :, :, cols].astype(f32).reshape(long + 2 * SUB, 128)
+                for b in range(3):
+                    seen = line[SUB + b - 1 : SUB + b - 1 + long]
+                    for a in range(3):
+                        o = r - a
+                        if 0 <= o < rows:
+                            tap = 3 * a + b if t == 0 else 8 - 3 * a - b
+                            term = weights[tap : tap + 1] * seen
+                            sums[o] = term if sums[o] is None else sums[o] + term
+            for o in range(rows):
+                conv[t, o, :, :, cols] = sums[o].reshape(groups, SUB, 128)
+        return carry
+
+    lax.fori_loop(0, width // 128, conv_step, 0)
+
+    for c in mine + own:
+        c.wait()
+    for d in col_order:
+        for t in range(4):
+            p = lax.rem(mc + d, C)
+            row_back(t, p, p).wait_recv()
+    for ch in range(CHUNKS):
+        for d in order:
+            for t in range(4):
+                p = lax.rem(me + d, R)
+                col_back(t, ch, p, p).wait_recv()
+    final_copies = [pltpu.make_async_copy(ret.at[t], outs_hbm[t], final.at[t]) for t in (1, 2)]
+    for c in final_copies:
+        c.start()
+
+    def add_step(n, carry):
+        cols = lanes(n * 128, 128)
+        for t, source in ((0, 0), (1, 3)):
+            done[t, :, :, :, cols] = (ret[source, :, :, :, cols].astype(f32) + conv[t, :, :, :, cols]).astype(jnp.bfloat16)
+        return carry
+
+    lax.fori_loop(0, width // 128, add_step, 0)
+    last = [pltpu.make_async_copy(done.at[t], outs_hbm[(0, 3)[t]], final.at[(0, 3)[t]]) for t in range(2)]
+    for c in last:
+        c.start()
+    for d in col_order:
+        for t in range(4):
+            p = lax.rem(mc + d, C)
+            row_in(t, p, p).wait_send()
+            row_back(t, p, p).wait_send()
+    for ch in range(CHUNKS):
+        for d in order:
+            for t in range(4):
+                p = lax.rem(me + d, R)
+                col_in(t, ch, p, p).wait_send()
+                col_back(t, ch, p, p).wait_send()
+    for t in range(2):
+        for i in range(8):
+            @pl.when(has(i, 1))
+            def _(t=t, i=i):
+                halo(t, i).wait_send()
+    for c in final_copies + last:
+        c.wait()
+
+
+def fused_body(query, key, value, cotangent, conv_weight, row_mask, col_mask):
+    rows, cols_here, width = query.shape
+    R, C = lax.axis_size("rows"), lax.axis_size("cols")
+    groups = cols_here // SUB
+    half = width // 2
+    share = half // C
+    length = R * rows * SUB
+    views = [x.reshape(rows, groups, SUB, width) for x in (query, key, value, cotangent)]
+    row_allow = jnp.repeat(row_mask.astype(jnp.float32), cols_here * C // SHEET_ROW_BLOCKS, axis=2)
+    tables = lax.dynamic_slice_in_dim(col_mask, lax.axis_index("rows") * SUB, SUB, 0)
+    spread = jnp.repeat(jnp.transpose(tables, (1, 0, 2)).astype(jnp.float32), length // COL_BLOCKS, axis=2)
+    same = lax.broadcasted_iota(jnp.int32, (1, SUB, length), 1) == lax.broadcasted_iota(jnp.int32, (1, SUB, length), 2) % SUB
+    col_allow = jnp.where(same, spread, 0.0)
+    bf16 = jnp.bfloat16
+    any_spec = pl.BlockSpec(memory_space=pl.ANY)
+    vmem = pl.BlockSpec(memory_space=pltpu.VMEM)
+    dma = pltpu.SemaphoreType.DMA
+    outs = pl.pallas_call(
+        functools.partial(layer_kernel, (R, C, rows, groups, width)),
+        out_shape=[jax.ShapeDtypeStruct((rows, groups, SUB, width), bf16)] * 4,
+        in_specs=[any_spec] * 4 + [vmem] * 3,
+        out_specs=[any_spec] * 4,
+        scratch_shapes=[
+            pltpu.VMEM((4, R, rows, SUB, half), bf16),
+            pltpu.VMEM((4, R, rows, SUB, half), bf16),
+            pltpu.VMEM((4, rows, C, groups, SUB, share), bf16),
+            pltpu.VMEM((4, rows, C, groups, SUB, share), bf16),
+            pltpu.VMEM((2, rows + 2, groups + 2, SUB, width), bf16),
+            pltpu.VMEM((2, rows, groups, SUB, width), jnp.float32),
+            pltpu.VMEM((4, rows, groups, SUB, width), bf16),
+            pltpu.VMEM((2, rows, groups, SUB, width), bf16),
+            dma((4, CHUNKS, R)), dma((4, CHUNKS, R)), dma((4, CHUNKS, R)), dma((4, CHUNKS, R)),
+            dma((4, C)), dma((4, C)), dma((4, C)), dma((4, C)),
+            dma((2, 8)), dma((2, 8)), dma((3, 4)), dma((4,)),
+        ],
+        compiler_params=pltpu.CompilerParams(collective_id=0, has_side_effects=True, vmem_limit_bytes=56 << 20),
+    )(*views, conv_weight, row_allow, col_allow)
+    return tuple(x.reshape(query.shape) for x in outs)
+
+
+def any_body(query, key, value, cotangent, conv_weight, row_mask, col_mask):
+    rows, cols_here, width = query.shape
+    R, C = lax.axis_size("rows"), lax.axis_size("cols")
+    fits = cols_here == R * SUB and (width // 2) % (C * HEAD_DIM) == 0
+    chosen = fused_body if fits else body
+    return chosen(query, key, value, cotangent, conv_weight, row_mask, col_mask)
+
+
 def solution(mesh):
     return jax.shard_map(
-        body,
+        any_body,
         mesh=mesh,
         in_specs=(
             P("rows", "cols", None),

time: 260 us -> 104 us (0.40)
  Pallas kernels: 0 us -> 94.3 us
  starting transfers between devices: 74.1 us -> 0 us
  local copies, waits for them, and re-layouts: 66.4 us -> 7.68 us
  waiting for transfers between devices: 49.7 us -> 0 us
  matrix products: 34 us -> 0 us
  other arithmetic: 18.9 us -> 0.71 us
  between operations: 14.3 us -> 0.69 us
    pallas_call x0 -> x1, Pallas kernels: none -> 94.3 us  [fused_body(): pl.pallas_call(functools.partial(layer_kernel, (R, C, rows, groups, width...]
    all_to_all x8 -> x0, starting transfers between devices: 46.6 us -> none  [the longest x1 6.59 us: body(): lax.all_to_all(cotangent[:, :, half_width:], 'rows', split_axis=1, concat...]
    dot_general x15 -> x0, matrix products: 34 us -> none  [the longest x2 10.4 us: line_attention(): jnp.einsum('bhqk,' + key_layout_shape + '->' + query_form, rounded, value...]
    all_gather x2 -> x0, waiting for transfers between devices: 33.6 us -> none  [the longest x1 17.9 us: body(): lax.all_gather(key[:, :, :half_width], 'cols', axis=1, tiled=True)]
    ppermute x8 -> x0, starting transfers between devices: 27.4 us -> none  [the longest x4 17.5 us: padded(): after = lax.ppermute(leading, axis, down)]
    all_to_all x8 -> x0, waiting for transfers between devices: 16 us -> none  [the longest x1 11.3 us: body(): lax.all_to_all(query[:, :, half_width:], 'rows', split_axis=1, concat_axi...]
    convert_element_type x5 -> x2, other arithmetic: 13.2 us -> 0.08 us  [the longest x1 0.07 us: fused_body(): jnp.transpose(tables, (1, 0, 2)).astype(jnp.float32)]
    convert_element_type x11 -> x2, local copies, waits for them, and re-layouts: 11.6 us -> 0.2 us  [the longest x1 0.1 us: fused_body(): row_mask.astype(jnp.float32)]
  transfers between devices with their start and end apart: 20 -> 0, of which waited for: 6 -> 0; matrix products, arithmetic and copies ran while one was open for 35% -> 0% of each run, Pallas kernels for 0% -> 0%
where the time goes in v1:
time: 104 us; the launch traced here: 103 us
  Pallas kernels  94.3 us (91%)
  local copies, waits for them, and re-layouts  7.68 us (7%)
    pallas_call x1, Pallas kernels, fused_body(): pl.pallas_call(functools.partial(layer_kernel, (R, C, rows, groups, width...  94.3 us
    unnamed x14, local copies, waits for them, and re-layouts  6.62 us

profile of v1, /device:TPU:17, one launch (start us, length us, event | category | flops | bytes accessed | tf_op | source)
XLA Modules:
  0.0 103.4 jit_solution(15628686774132243457)
XLA Ops:
  0.6 0.0 copy-start.4
  0.7 0.7 copy-done.4
  1.3 0.1 copy.13
  1.4 0.1 broadcast_in_dim.18
  1.5 0.0 copy-start.3
  1.5 0.6 reshape.94.row_allow
  2.1 0.1 copy-done.3
  2.2 0.1 convert_bitcast_fusion
  2.3 0.1 copy.14
  2.4 0.1 broadcast_in_dim.20
  2.5 0.1 reshape.95
  2.6 0.6 broadcast_select_fusion.col_allow
  3.2 94.3 %shard_map.102 = (bf16[3,8,8,2048]{3,2,1,0:T(8,128)(2,1)}, bf16[3,8,8,2048]{3,2,1,0:T(8,128)(2,1)}, bf16[3,8,8,2048]{3,2,1,0:T(8,128)(2,1)}, bf16[3,8,8,2048]{3,2,1,0:T(8,128)(2,1)}) custom-call(bf16[3,8,8,2048]{3,2,1,0:T(8,128)(2,1)} %bitcast.14, bf16[3,8,8,2048]{3,2,1,0:T(8,128)(2,1)} %bitcast.15, bf16[3,8,8,2048]{3,2,1,0:T(8,128)(2,1)} %bitcast.16, ...), custom_call_target="tpu_custom_call" | custom-call | tf_op jit(solution)/shard_map/pallas_call | solution.py:491
  97.5 0.0 copy-start.2
  97.5 2.2 %copy.19 = bf16[3,64,2048]{2,1,0:T(8,128)(2,1)} copy(bf16[3,64,2048]{2,1,0:T(8,128)(2,1)} %bitcast.13) | data formatting | bytes 1572864
  99.7 0.0 copy-done.2
  99.7 0.0 copy-start.1
  99.7 0.9 copy.20
  100.6 0.5 copy-done.1
  101.1 0.0 copy-start
  101.1 0.9 copy.21
  102.0 0.5 copy-done
  102.5 0.9 copy.22
  (4 shorter events, 0.0 us)
Async XLA Ops:
  0.6 0.7 copy-start.4
  1.5 0.7 copy-start.3
  97.5 2.2 %copy-start.2 = (bf16[3,8,8,2048]{3,2,1,0:T(8,128)(2,1)S(1)}, bf16[3,8,8,2048]{3,2,1,0:T(8,128)(2,1)}, u32[]{:S(2)}) copy-start(bf16[3,8,8,2048]{3,2,1,0:T(8,128)(2,1)} %get-tuple-element.9) | copy-start | bytes 2359300
  99.7 1.4 %copy-start.1 = (bf16[3,8,8,2048]{3,2,1,0:T(8,128)(2,1)S(1)}, bf16[3,8,8,2048]{3,2,1,0:T(8,128)(2,1)}, u32[]{:S(2)}) copy-start(bf16[3,8,8,2048]{3,2,1,0:T(8,128)(2,1)} %get-tuple-element.10) | copy-start | bytes 2359300
  101.1 1.4 %copy-start = (bf16[3,8,8,2048]{3,2,1,0:T(8,128)(2,1)S(1)}, bf16[3,8,8,2048]{3,2,1,0:T(8,128)(2,1)}, u32[]{:S(2)}) copy-start(bf16[3,8,8,2048]{3,2,1,0:T(8,128)(2,1)} %get-tuple-element.11) | copy-start | bytes 2359300

commit v2 on v1

--- a/solution.py
+++ b/solution.py
@@ -215,12 +215,11 @@
 
 
 def layer_kernel(
-    dims, q_hbm, k_hbm, v_hbm, g_hbm, taps, row_allow, col_allow, *rest
+    dims, q_hbm, k_hbm, v_hbm, g_hbm, taps, row_mask, col_mask, ret, conv_hbm, *rest
 ):
     R, C, rows, groups, width = dims
-    outs_hbm = rest[:4]
-    colbuf, colout, rowbuf, rowout, ext, conv, ret, done = rest[4:12]
-    (ci_s, ci_r, co_s, co_r, ri_s, ri_r, ro_s, ro_r, ha_s, ha_r, local, final) = rest[12:]
+    colbuf, colout, rowbuf, rowout, ext, conv, hop = rest[:7]
+    (ci_s, ci_r, co_s, co_r, ri_s, ri_r, ro_s, ro_r, ha_s, ha_r, local) = rest[7:]
     half = width // 2
     share = half // C
     part = half // CHUNKS
@@ -260,55 +259,45 @@
             send_sem=ro_s.at[t, p], recv_sem=ro_r.at[t, slot],
             device_id={"cols": p}, device_id_type=MESH)
 
-    def row_span(dr, there):
-        if dr == 0:
-            return pl.ds(1, rows) if there else pl.ds(0, rows)
-        if dr == 1:
-            return pl.ds(0, 1) if there else pl.ds(rows - 1, 1)
-        return pl.ds(rows + 1, 1) if there else pl.ds(0, 1)
-
-    def group_span(dc, there):
-        if dc == 0:
-            return pl.ds(1, groups) if there else pl.ds(0, groups)
-        if dc == 1:
-            return pl.ds(0, 1) if there else pl.ds(groups - 1, 1)
-        return pl.ds(groups + 1, 1) if there else pl.ds(0, 1)
-
-    directions = [(a, b) for a in (-1, 0, 1) for b in (-1, 0, 1) if (a, b) != (0, 0)]
-
-    def halo(t, i):
-        dr, dc = directions[i]
+    odd = lax.rem(me, 2)
+    sign = 2 * odd - 1
+    crosses = jnp.logical_and(me + sign >= 0, me + sign < R)
+    relays = jnp.logical_and(me - 2 * sign >= 0, me - 2 * sign < R)
+    inner = pl.ds(1, groups)
+
+    def halo(kind, t, src, dst, target):
         return pltpu.make_async_remote_copy(
-            src_ref=inputs[2 + t].at[row_span(dr, False), group_span(dc, False)],
-            dst_ref=ext.at[t, row_span(dr, True), group_span(dc, True)],
-            send_sem=ha_s.at[t, i], recv_sem=ha_r.at[t, i],
-            device_id={"rows": me + dr, "cols": mc + dc}, device_id_type=MESH)
-
-    def has(i, sign):
-        dr, dc = directions[i]
-        conds = []
-        if sign * dr == 1:
-            conds.append(me < R - 1)
-        if sign * dr == -1:
-            conds.append(me > 0)
-        if sign * dc == 1:
-            conds.append(mc < C - 1)
-        if sign * dc == -1:
-            conds.append(mc > 0)
-        ok = conds[0]
-        for c in conds[1:]:
-            ok = jnp.logical_and(ok, c)
-        return ok
+            src_ref=src, dst_ref=dst, send_sem=ha_s.at[kind, t], recv_sem=ha_r.at[kind, t],
+            device_id=target, device_id_type=MESH)
+
+    def cross(t, slot):
+        return halo(0, t, inputs[2 + t].at[odd * (rows - 1), :, :, pl.ds(0, half)],
+                    ext.at[t, slot, inner, :, pl.ds(0, half)], {"rows": me + sign})
+
+    def detour(t):
+        return halo(1, t, inputs[2 + t].at[odd * (rows - 1), :, :, pl.ds(half, half)],
+                    hop.at[t], {"rows": me + 2 * sign})
+
+    def forward(t, slot):
+        return halo(2, t, hop.at[t], ext.at[t, slot, inner, :, pl.ds(half, half)], {"rows": me - sign})
+
+    def near(t, slot):
+        return halo(3, t, inputs[2 + t].at[(1 - odd) * (rows - 1)], ext.at[t, slot, inner], {"rows": me - sign})
+
+    def rightward(t):
+        return halo(4, t, ext.at[t, :, groups], ext.at[t, :, 0], {"cols": mc + 1})
+
+    def leftward(t):
+        return halo(5, t, ext.at[t, :, 1], ext.at[t, :, groups + 1], {"cols": mc - 1})
+
+    even_slot, odd_slot = (1 - odd) * (rows + 1), odd * (rows + 1)
 
     barrier = pltpu.get_barrier_semaphore()
     for d in range(1, R):
         pl.semaphore_signal(barrier, inc=1, device_id={"rows": lax.rem(me + d, R)}, device_id_type=MESH)
     for d in range(1, C):
         pl.semaphore_signal(barrier, inc=1, device_id={"cols": lax.rem(mc + d, C)}, device_id_type=MESH)
-    for dr, dc in ((1, 1), (1, -1), (-1, 1), (-1, -1)):
-        corner = {"rows": lax.rem(me + dr + R, R), "cols": lax.rem(mc + dc + C, C)}
-        pl.semaphore_signal(barrier, inc=1, device_id=corner, device_id_type=MESH)
-    pl.semaphore_wait(barrier, R - 1 + C - 1 + 4)
+    pl.semaphore_wait(barrier, R - 1 + C - 1)
 
     order = sorted(range(1, R), key=lambda d: abs(d - R / 2))
     col_order = sorted(range(1, C), key=lambda d: abs(d - C / 2))
@@ -319,11 +308,13 @@
         for d in order:
             for t in range(4):
                 col_in(t, ch, lax.rem(me + d, R), me).start()
+    @pl.when(crosses)
+    def _():
+        for t in range(2):
+            detour(t).start()
+            cross(t, even_slot).start()
     for t in range(2):
-        for i in range(8):
-            @pl.when(has(i, 1))
-            def _(t=t, i=i):
-                halo(t, i).start()
+        near(t, odd_slot).start()
 
     mine = []
     for t in range(4):
@@ -333,15 +324,32 @@
         mine.append(pltpu.make_async_copy(inputs[2 + t], ext.at[t, pl.ds(1, rows), pl.ds(1, groups)], local.at[2, t]))
     for c in mine:
         c.start()
-    for t in range(2):
-        for i in range(8):
-            @pl.when(jnp.logical_not(has(i, -1)))
-            def _(t=t, i=i):
-                dr, dc = directions[i]
-                view = ext.at[t, row_span(dr, True), group_span(dc, True)]
-                view[...] = jnp.zeros(view.shape, view.dtype)
+    for edge, area in (
+        (me == 0, (slice(None), 0, inner)),
+        (me == R - 1, (slice(None), rows + 1, inner)),
+        (mc == 0, (slice(None), slice(None), 0)),
+        (mc == C - 1, (slice(None), slice(None), groups + 1)),
+    ):
+        @pl.when(edge)
+        def _(area=area):
+            view = ext.at[area]
+            view[...] = jnp.zeros(view.shape, view.dtype)
     for c in mine:
         c.wait()
+
+    length = R * rows * SUB
+    col_size = length // COL_BLOCKS
+    key_pos = lax.broadcasted_iota(jnp.int32, (SUB, length), 1)
+    lane_col = lax.broadcasted_iota(jnp.int32, (SUB, length), 0)
+    block = jnp.where(lax.rem(key_pos, SUB) == lane_col, key_pos // col_size, -1)
+    col_tables = []
+    for b in range(COL_BLOCKS):
+        table = jnp.zeros((SUB, length), jnp.int32)
+        for c in range(SUB):
+            for j in range(COL_BLOCKS):
+                here = jnp.logical_and(lane_col == c, block == j)
+                table = jnp.where(here, col_mask[me * SUB + c, b, j], table)
+        col_tables.append(table)
 
     for d in col_order:
         for t in range(4):
@@ -353,10 +361,15 @@
         i, h = n // (share // HEAD_DIM), lax.rem(n, share // HEAD_DIM)
         cols = lanes(h * HEAD_DIM, HEAD_DIM)
         x = [rowbuf[t, i, :, :, :, cols].astype(f32).reshape(tokens, HEAD_DIM).astype(jnp.bfloat16) for t in range(4)]
-        table = row_allow[i]
         size = tokens // SHEET_ROW_BLOCKS
-        allow = jnp.concatenate(
-            [jnp.broadcast_to(table[b : b + 1], (size, tokens)) for b in range(SHEET_ROW_BLOCKS)], axis=0) > 0.5
+        place = lax.broadcasted_iota(jnp.int32, (SUB, tokens), 1) // size
+        bands = []
+        for b in range(SHEET_ROW_BLOCKS):
+            table = jnp.zeros((SUB, tokens), jnp.int32)
+            for j in range(SHEET_ROW_BLOCKS):
+                table = jnp.where(place == j, row_mask[i, b, j], table)
+            bands.append(jnp.broadcast_to(table[None], (size // SUB, SUB, tokens)).reshape(size, tokens))
+        allow = jnp.concatenate(bands, axis=0) > 0
         for t, y in enumerate(attend(*x, allow)):
             rowout[t, i, :, :, :, cols] = y.reshape(C, groups, SUB, HEAD_DIM).astype(jnp.bfloat16)
         return carry
@@ -369,15 +382,13 @@
     for c in mine:
         c.start()
 
-    length = R * rows * SUB
-    col_size = length // COL_BLOCKS
     for ch in range(CHUNKS):
         for d in order:
             for t in range(4):
                 p = lax.rem(me + d, R)
                 col_in(t, ch, p, p).wait_recv()
         allow = jnp.concatenate(
-            [jnp.broadcast_to(col_allow[b][None], (col_size // SUB, SUB, length)).reshape(col_size, length) for b in range(COL_BLOCKS)], axis=0) > 0.5
+            [jnp.broadcast_to(t[None], (col_size // SUB, SUB, length)).reshape(col_size, length) for t in col_tables], axis=0) > 0
 
         def col_step(h, carry):
             cols = lanes(ch * part + h * HEAD_DIM, HEAD_DIM)
@@ -394,15 +405,39 @@
     for c in own:
         c.start()
 
+    @pl.when(relays)
+    def _():
+        for t in range(2):
+            detour(t).wait_recv()
+            forward(t, even_slot).start()
     for t in range(2):
-        for i in range(8):
-            @pl.when(has(i, -1))
-            def _(t=t, i=i):
-                pltpu.make_async_remote_copy(
-                    src_ref=inputs[2 + t].at[row_span(directions[i][0], False), group_span(directions[i][1], False)],
-                    dst_ref=ext.at[t, row_span(directions[i][0], True), group_span(directions[i][1], True)],
-                    send_sem=ha_s.at[t, i], recv_sem=ha_r.at[t, i],
-                    device_id={"rows": me - directions[i][0], "cols": mc - directions[i][1]}, device_id_type=MESH).wait_recv()
+        near(t, even_slot).wait_recv()
+
+    @pl.when(crosses)
+    def _():
+        for t in range(2):
+            cross(t, odd_slot).wait_recv()
+            forward(t, odd_slot).wait_recv()
+
+    @pl.when(mc < C - 1)
+    def _():
+        for t in range(2):
+            rightward(t).start()
+
+    @pl.when(mc > 0)
+    def _():
+        for t in range(2):
+            leftward(t).start()
+
+    @pl.when(mc > 0)
+    def _():
+        for t in range(2):
+            rightward(t).wait_recv()
+
+    @pl.when(mc < C - 1)
+    def _():
+        for t in range(2):
+            leftward(t).wait_recv()
     long = groups * SUB
 
     def conv_step(n, carry):
@@ -425,6 +460,8 @@
         return carry
 
     lax.fori_loop(0, width // 128, conv_step, 0)
+    keep = pltpu.make_async_copy(conv, conv_hbm, local.at[2, 2])
+    keep.start()
 
     for c in mine + own:
         c.wait()
@@ -437,20 +474,6 @@
             for t in range(4):
                 p = lax.rem(me + d, R)
                 col_back(t, ch, p, p).wait_recv()
-    final_copies = [pltpu.make_async_copy(ret.at[t], outs_hbm[t], final.at[t]) for t in (1, 2)]
-    for c in final_copies:
-        c.start()
-
-    def add_step(n, carry):
-        cols = lanes(n * 128, 128)
-        for t, source in ((0, 0), (1, 3)):
-            done[t, :, :, :, cols] = (ret[source, :, :, :, cols].astype(f32) + conv[t, :, :, :, cols]).astype(jnp.bfloat16)
-        return carry
-
-    lax.fori_loop(0, width // 128, add_step, 0)
-    last = [pltpu.make_async_copy(done.at[t], outs_hbm[(0, 3)[t]], final.at[(0, 3)[t]]) for t in range(2)]
-    for c in last:
-        c.start()
     for d in col_order:
         for t in range(4):
             p = lax.rem(mc + d, C)
@@ -463,12 +486,36 @@
                 col_in(t, ch, p, p).wait_send()
                 col_back(t, ch, p, p).wait_send()
     for t in range(2):
-        for i in range(8):
-            @pl.when(has(i, 1))
-            def _(t=t, i=i):
-                halo(t, i).wait_send()
-    for c in final_copies + last:
-        c.wait()
+        near(t, odd_slot).wait_send()
+
+    @pl.when(crosses)
+    def _():
+        for t in range(2):
+            cross(t, even_slot).wait_send()
+            detour(t).wait_send()
+
+    @pl.when(relays)
+    def _():
+        for t in range(2):
+            forward(t, even_slot).wait_send()
+
+    @pl.when(mc < C - 1)
+    def _():
+        for t in range(2):
+            rightward(t).wait_send()
+
+    @pl.when(mc > 0)
+    def _():
+        for t in range(2):
+            leftward(t).wait_send()
+    keep.wait()
+
+
+def finish_kernel(ret, conv, out, dquery, dkey, dvalue):
+    out[...] = (ret[0].astype(jnp.float32) + conv[0]).astype(jnp.bfloat16)
+    dquery[...] = ret[1]
+    dkey[...] = ret[2]
+    dvalue[...] = (ret[3].astype(jnp.float32) + conv[1]).astype(jnp.bfloat16)
 
 
 def fused_body(query, key, value, cotangent, conv_weight, row_mask, col_mask):
@@ -477,22 +524,17 @@
     groups = cols_here // SUB
     half = width // 2
     share = half // C
-    length = R * rows * SUB
     views = [x.reshape(rows, groups, SUB, width) for x in (query, key, value, cotangent)]
-    row_allow = jnp.repeat(row_mask.astype(jnp.float32), cols_here * C // SHEET_ROW_BLOCKS, axis=2)
-    tables = lax.dynamic_slice_in_dim(col_mask, lax.axis_index("rows") * SUB, SUB, 0)
-    spread = jnp.repeat(jnp.transpose(tables, (1, 0, 2)).astype(jnp.float32), length // COL_BLOCKS, axis=2)
-    same = lax.broadcasted_iota(jnp.int32, (1, SUB, length), 1) == lax.broadcasted_iota(jnp.int32, (1, SUB, length), 2) % SUB
-    col_allow = jnp.where(same, spread, 0.0)
     bf16 = jnp.bfloat16
     any_spec = pl.BlockSpec(memory_space=pl.ANY)
     vmem = pl.BlockSpec(memory_space=pltpu.VMEM)
     dma = pltpu.SemaphoreType.DMA
-    outs = pl.pallas_call(
+    smem = pl.BlockSpec(memory_space=pltpu.SMEM)
+    ret, conv = pl.pallas_call(
         functools.partial(layer_kernel, (R, C, rows, groups, width)),
-        out_shape=[jax.ShapeDtypeStruct((rows, groups, SUB, width), bf16)] * 4,
-        in_specs=[any_spec] * 4 + [vmem] * 3,
-        out_specs=[any_spec] * 4,
+        out_shape=[jax.ShapeDtypeStruct((4, rows, groups, SUB, width), bf16), jax.ShapeDtypeStruct((2, rows, groups, SUB, width), jnp.float32)],
+        in_specs=[any_spec] * 4 + [vmem, smem, smem],
+        out_specs=[any_spec] * 2,
         scratch_shapes=[
             pltpu.VMEM((4, R, rows, SUB, half), bf16),
             pltpu.VMEM((4, R, rows, SUB, half), bf16),
@@ -500,21 +542,32 @@
             pltpu.VMEM((4, rows, C, groups, SUB, share), bf16),
             pltpu.VMEM((2, rows + 2, groups + 2, SUB, width), bf16),
             pltpu.VMEM((2, rows, groups, SUB, width), jnp.float32),
-            pltpu.VMEM((4, rows, groups, SUB, width), bf16),
-            pltpu.VMEM((2, rows, groups, SUB, width), bf16),
+            pltpu.VMEM((2, groups, SUB, half), bf16),
             dma((4, CHUNKS, R)), dma((4, CHUNKS, R)), dma((4, CHUNKS, R)), dma((4, CHUNKS, R)),
             dma((4, C)), dma((4, C)), dma((4, C)), dma((4, C)),
-            dma((2, 8)), dma((2, 8)), dma((3, 4)), dma((4,)),
+            dma((6, 2)), dma((6, 2)), dma((3, 4)),
         ],
         compiler_params=pltpu.CompilerParams(collective_id=0, has_side_effects=True, vmem_limit_bytes=56 << 20),
-    )(*views, conv_weight, row_allow, col_allow)
+    )(*views, conv_weight, row_mask, col_mask)
+    split = 2
+    one = pl.BlockSpec((1, groups, SUB, width // split), lambda i, j: (i, 0, 0, j))
+    outs = pl.pallas_call(
+        finish_kernel,
+        out_shape=[jax.ShapeDtypeStruct((rows, groups, SUB, width), bf16)] * 4,
+        grid=(rows, split),
+        in_specs=[
+            pl.BlockSpec((4, 1, groups, SUB, width // split), lambda i, j: (0, i, 0, 0, j)),
+            pl.BlockSpec((2, 1, groups, SUB, width // split), lambda i, j: (0, i, 0, 0, j)),
+        ],
+        out_specs=[one] * 4,
+    )(ret, conv)
     return tuple(x.reshape(query.shape) for x in outs)
 
 
 def any_body(query, key, value, cotangent, conv_weight, row_mask, col_mask):
     rows, cols_here, width = query.shape
     R, C = lax.axis_size("rows"), lax.axis_size("cols")
-    fits = cols_here == R * SUB and (width // 2) % (C * HEAD_DIM) == 0
+    fits = R % 2 == 0 and cols_here == R * SUB and (width // 2) % (C * HEAD_DIM) == 0
     chosen = fused_body if fits else body
     return chosen(query, key, value, cotangent, conv_weight, row_mask, col_mask)
 

time: 104 us -> 100 us (0.962)
  local copies, waits for them, and re-layouts: 7.68 us -> 2.81 us
    pallas_call x0 -> x1, Pallas kernels: none -> 5.89 us  [fused_body(): pl.pallas_call(finish_kernel, out_shape=[jax.ShapeDtypeStruct((rows, grou...]
    pallas_call x1, Pallas kernels: 94.3 us -> 89.1 us  [fused_body(): pl.pallas_call(functools.partial(layer_kernel, (R, C, rows, groups, width...]
    unnamed x14 -> x2, local copies, waits for them, and re-layouts: 6.62 us -> 2.81 us
where the time goes in v2:
time: 100 us; the launch traced here: 98.4 us
  Pallas kernels  95 us (95%)
  local copies, waits for them, and re-layouts  2.81 us (3%)
    pallas_call x1, Pallas kernels, fused_body(): pl.pallas_call(functools.partial(layer_kernel, (R, C, rows, groups, width...  89.1 us
    pallas_call x1, Pallas kernels, fused_body(): pl.pallas_call(finish_kernel, out_shape=[jax.ShapeDtypeStruct((rows, grou...  5.89 us
    unnamed x2, local copies, waits for them, and re-layouts  2.81 us

profile of v2, /device:TPU:17, one launch (start us, length us, event | category | flops | bytes accessed | tf_op | source)
XLA Modules:
  0.0 98.4 jit_solution(13162490225303600593)
XLA Ops:
  0.6 1.3 %copy.11.row_mask = s32[3,2,2]{2,1,0:T(2,128)} copy(s32[3,2,2]{0,2,1:T(2,128)} %param.12) | data formatting | bytes 96 | tf_op args[5]
  2.0 1.5 %copy.12.col_mask = s32[64,3,3]{2,1,0:T(4,128)} copy(s32[64,3,3]{0,2,1:T(4,128)} %param.13) | data formatting | bytes 4608 | tf_op args[6]
  3.4 89.1 %shard_map.102 = (bf16[4,3,8,8,2048]{4,3,2,1,0:T(8,128)(2,1)}, f32[2,3,8,8,2048]{4,3,2,1,0:T(8,128)}) custom-call(bf16[3,8,8,2048]{3,2,1,0:T(8,128)(2,1)} %bitcast.8, bf16[3,8,8,2048]{3,2,1,0:T(8,128)(2,1)} %bitcast.9, bf16[3,8,8,2048]{3,2,1,0:T(8,128)(2,1)} %bitcast.10, bf16[3,8,8,2048]{3,2,1,0:T(8,128)(2,1)} %bitcast.11, bf16[9,2048]{1,0:T(8,128)(2,1)} %taps.1, ...), custom_call_target="tpu_custom_call" | custom-call | tf_op jit(solution)/shard_map/pallas_call | solution.py:533
  92.5 5.9 %shard_map.103 = (bf16[3,8,8,2048]{3,2,1,0:T(8,128)(2,1)}, bf16[3,8,8,2048]{3,2,1,0:T(8,128)(2,1)}, bf16[3,8,8,2048]{3,2,1,0:T(8,128)(2,1)}, bf16[3,8,8,2048]{3,2,1,0:T(8,128)(2,1)}) custom-call(bf16[4,3,8,8,2048]{4,3,2,1,0:T(8,128)(2,1)} %get-tuple-element.10.ret, f32[2,3,8,8,2048]{4,3,2,1,0:T(8,128)} %get-tuple-element.11.conv), custom_call_target="tpu_custom_call" | custom-call | tf_op jit(solution)/shard_map/pallas_call | solution.py:554

commit v3 on v2

--- a/solution.py
+++ b/solution.py
@@ -193,7 +193,7 @@
 
 
 SUB = 8
-CHUNKS = 2
+CHUNKS = 1
 MESH = pl.DeviceIdType.MESH
 
 
@@ -348,7 +348,7 @@
         for c in range(SUB):
             for j in range(COL_BLOCKS):
                 here = jnp.logical_and(lane_col == c, block == j)
-                table = jnp.where(here, col_mask[me * SUB + c, b, j], table)
+                table = jnp.where(here, col_mask[b, j, me * SUB + c], table)
         col_tables.append(table)
 
     for d in col_order:
@@ -367,7 +367,7 @@
         for b in range(SHEET_ROW_BLOCKS):
             table = jnp.zeros((SUB, tokens), jnp.int32)
             for j in range(SHEET_ROW_BLOCKS):
-                table = jnp.where(place == j, row_mask[i, b, j], table)
+                table = jnp.where(place == j, row_mask[b, j, i], table)
             bands.append(jnp.broadcast_to(table[None], (size // SUB, SUB, tokens)).reshape(size, tokens))
         allow = jnp.concatenate(bands, axis=0) > 0
         for t, y in enumerate(attend(*x, allow)):
@@ -548,7 +548,7 @@
             dma((6, 2)), dma((6, 2)), dma((3, 4)),
         ],
         compiler_params=pltpu.CompilerParams(collective_id=0, has_side_effects=True, vmem_limit_bytes=56 << 20),
-    )(*views, conv_weight, row_mask, col_mask)
+    )(*views, conv_weight, jnp.transpose(row_mask, (1, 2, 0)), jnp.transpose(col_mask, (1, 2, 0)))
     split = 2
     one = pl.BlockSpec((1, groups, SUB, width // split), lambda i, j: (i, 0, 0, j))
     outs = pl.pallas_call(

time: 100 us -> 93.8 us (0.938)
  Pallas kernels: 95 us -> 91.9 us
  local copies, waits for them, and re-layouts: 2.81 us -> 0 us
    pallas_call x1, Pallas kernels: 89.1 us -> 86.1 us  [fused_body(): pl.pallas_call(functools.partial(layer_kernel, (R, C, rows, groups, width...]
    unnamed x2 -> x0, local copies, waits for them, and re-layouts: 2.81 us -> none
where the time goes in v3:
time: 93.8 us; the launch traced here: 92.6 us
  Pallas kernels  91.9 us (98%)
    pallas_call x1, Pallas kernels, fused_body(): pl.pallas_call(functools.partial(layer_kernel, (R, C, rows, groups, width...  86.1 us
    pallas_call x1, Pallas kernels, fused_body(): pl.pallas_call(finish_kernel, out_shape=[jax.ShapeDtypeStruct((rows, grou...  5.89 us

profile of v3, /device:TPU:17, one launch (start us, length us, event | category | flops | bytes accessed | tf_op | source)
XLA Modules:
  0.0 92.6 jit_solution(10825578236970908245)
XLA Ops:
  0.6 86.1 %shard_map.102 = (bf16[4,3,8,8,2048]{4,3,2,1,0:T(8,128)(2,1)}, f32[2,3,8,8,2048]{4,3,2,1,0:T(8,128)}) custom-call(bf16[3,8,8,2048]{3,2,1,0:T(8,128)(2,1)} %bitcast.10, bf16[3,8,8,2048]{3,2,1,0:T(8,128)(2,1)} %bitcast.11, bf16[3,8,8,2048]{3,2,1,0:T(8,128)(2,1)} %bitcast.12, bf16[3,8,8,2048]{3,2,1,0:T(8,128)(2,1)} %bitcast.13, bf16[9,2048]{1,0:T(8,128)(2,1)} %taps.1, ...), custom_call_target="tpu_custom_call" | custom-call | tf_op jit(solution)/shard_map/pallas_call | solution.py:533
  86.7 5.9 %shard_map.103 = (bf16[3,8,8,2048]{3,2,1,0:T(8,128)(2,1)}, bf16[3,8,8,2048]{3,2,1,0:T(8,128)(2,1)}, bf16[3,8,8,2048]{3,2,1,0:T(8,128)(2,1)}, bf16[3,8,8,2048]{3,2,1,0:T(8,128)(2,1)}) custom-call(bf16[4,3,8,8,2048]{4,3,2,1,0:T(8,128)(2,1)} %get-tuple-element.10.ret, f32[2,3,8,8,2048]{4,3,2,1,0:T(8,128)} %get-tuple-element.11.conv), custom_call_target="tpu_custom_call" | custom-call | tf_op jit(solution)/shard_map/pallas_call | solution.py:554
